TPU v7x, 256 devices: a whole 4x4x8 slice. The times are simulated.
256 devices in a mesh: group: 4 (over x), leaf: 64 (over z, y, core).
Axes of the slice: x: 4, y: 4, z: 8, core: 2. Of those that a mesh axis runs over, the one named last changes fastest.
Arguments:
- right_sides: float32 [16, 1048576], P(None, ('group', 'leaf')), may hold values from -6 to 6
- near_blocks: float32 [16384, 8, 4096], P(('group', 'leaf')), may hold values from -0.375 to 0.375
- near_source: int32 [16384, 8], P(('group', 'leaf')), may hold values from 0 to 16383, as said below
- near_count: int32 [16384], P(('group', 'leaf')), may hold values from 1 to 8
- basis: float32 [16384, 2048], P(('group', 'leaf')), may hold values from -0.75 to 0.75
- leaf_source: int32 [16384, 8], P(('group', 'leaf')), may hold values from 0 to 16383
- leaf_coupling: float32 [16384, 8, 1024], P(('group', 'leaf')), may hold values from -0.375 to 0.375
- leaf_transfer: float32 [16384, 1024], P(('group', 'leaf')), may hold values from -1 to 1
- cluster_source: int32 [1024, 8], P(('group', 'leaf')), may hold values from 0 to 255
- cluster_coupling: float32 [1024, 8, 1024], P(('group', 'leaf')), may hold values from -0.09375 to 0.09375
- cluster_transfer: float32 [1024, 1024], P(('group', 'leaf')), may hold values from -1 to 1
- group_coupling: float32 [4, 4, 1024], P('group'), may hold values from -0.0078125 to 0.0078125
Outputs:
- applied: float32 [16, 1048576], P(None, ('group', 'leaf'))
Inputs may be any that keep to these rules, and one draw needn't show every extreme that they name: near_source[t, j] and leaf_source[t, j] name a leaf held by the same device as t or by the device just before or after it in the order of devices.
All inputs are finite; a program needn't handle non-finite values.
Results may differ from a plain program's by a relative error of at most 0.0001.
Values sent between devices are 32-bit elements; how exact they have to be, the bound alone decides.
No kernel may reach another device: no remote copies, remote signals or barrier semaphores. Data moves between devices by JAX's collectives and lax.ppermute only.
A program may use at most 128 MiB of HBM per device.

v0:
```python
import jax
import jax.numpy as jnp
from jax import lax
from jax.sharding import PartitionSpec as P

LEAF = 64
K = 32
RHS = 16
FAR0 = 8
FAR1 = 8
highest_precision = lax.Precision.HIGHEST


def extended(value, sides, width):
    for axis, dim in sides:
        size, length = (lax.axis_size(axis), value.shape[dim])
        up = [(i, (i + 1) % size) for i in range(size - 1)]
        down = [(j, i) for i, j in up]
        last = lax.slice_in_dim(value, length - width, length, axis=dim)
        leading = lax.slice_in_dim(value, 0, width, axis=dim)
        before = lax.ppermute(last, axis, up)
        after = lax.ppermute(leading, axis, down)
        value = jnp.concatenate([before, value, after], axis=dim)
    return value


def per_device(
    right_sides,
    near_blocks,
    near_source,
    near_count,
    basis,
    leaf_source,
    leaf_coupling,
    leaf_transfer,
    cluster_source,
    cluster_coupling,
    cluster_transfer,
    group_coupling,
):
    leaves_here = near_blocks.shape[0]
    clusters_here = cluster_coupling.shape[0]
    ngroups = lax.axis_size("group")
    device = lax.axis_index(("group", "leaf"))
    blocks = right_sides.reshape(RHS, leaves_here, LEAF).transpose(1, 0, 2)
    bases = basis.reshape(leaves_here, K, LEAF)
    leaf_coef = jnp.einsum("tka,tra->tkr", bases, blocks, precision=highest_precision)
    coef_rows = leaf_coef.transpose(2, 0, 1).reshape(RHS, leaves_here * K)
    point_ext = extended(right_sides, ((("group", "leaf"), 1),), leaves_here * LEAF)
    coef_ext = extended(coef_rows, ((("group", "leaf"), 1),), leaves_here * K)
    window_start = (device - 1) * leaves_here
    near_local = near_source - window_start
    point_blocks = point_ext.reshape(RHS, 3 * leaves_here, LEAF).transpose(1, 0, 2)
    busiest = jnp.max(near_count)

    def near_step(slot_index, running):
        picked = jnp.take(point_blocks, near_local[:, slot_index], axis=0)
        slab = lax.dynamic_index_in_dim(near_blocks, slot_index, axis=1, keepdims=False).reshape(
            leaves_here, LEAF, LEAF
        )
        live = (near_count > slot_index).astype(jnp.float32)
        term = jnp.einsum("tab,trb->tra", slab, picked, precision=highest_precision)
        return running + term * live[:, None, None]

    near_total = lax.fori_loop(
        0, busiest, near_step, jnp.zeros((leaves_here, RHS, LEAF), jnp.float32)
    )
    coef_blocks = coef_ext.reshape(RHS, 3 * leaves_here, K)
    picked_coef = jnp.take(coef_blocks, leaf_source - window_start, axis=1)
    leaf_far = jnp.einsum(
        "tjkl,rtjl->tkr",
        leaf_coupling.reshape(leaves_here, FAR0, K, K),
        picked_coef,
        precision=highest_precision,
    )
    transfers = leaf_transfer.reshape(leaves_here, K, K)
    lifted = jnp.einsum("tkl,tlr->tkr", transfers, leaf_coef, precision=highest_precision)
    cluster_coef = lifted.reshape(clusters_here, leaves_here // clusters_here, K, RHS).sum(axis=1)
    cluster_rows = cluster_coef.reshape(clusters_here, K * RHS)
    couplings = cluster_coupling.reshape(clusters_here, FAR1, K, K)
    shard_rows = lax.all_gather(cluster_rows, "leaf", axis=0, tiled=True)
    onehot = (cluster_source[:, :, None] == jnp.arange(shard_rows.shape[0])[None, None, :]).astype(
        jnp.float32
    )
    selected = jnp.einsum("ujn,nm->ujm", onehot, shard_rows, precision=highest_precision)
    selected = selected.reshape(clusters_here, FAR1, K, RHS)
    cluster_far = jnp.einsum("ujkl,ujlr->ukr", couplings, selected, precision=highest_precision)
    upper = cluster_transfer.reshape(clusters_here, K, K)
    projected = jnp.einsum("ukl,ulr->ukr", upper, cluster_coef, precision=highest_precision)
    projected_sum = projected.sum(axis=0).reshape(1, K * RHS)
    group_sum = lax.psum(projected_sum, "leaf")
    all_groups = lax.all_gather(group_sum, "group", axis=0, tiled=True)
    group_field = jnp.einsum(
        "hkl,hlr->kr",
        group_coupling.reshape(ngroups, K, K),
        all_groups.reshape(ngroups, K, RHS),
        precision=highest_precision,
    )
    cluster_field = cluster_far + jnp.einsum(
        "ulk,lr->ukr", upper, group_field, precision=highest_precision
    )
    spread_cluster = jnp.repeat(cluster_field, leaves_here // clusters_here, axis=0)
    leaf_field = leaf_far + jnp.einsum(
        "tlk,tlr->tkr", transfers, spread_cluster, precision=highest_precision
    )
    total = near_total + jnp.einsum("tka,tkr->tra", bases, leaf_field, precision=highest_precision)
    return total.transpose(1, 0, 2).reshape(RHS, leaves_here * LEAF)


def solution(mesh):
    in_specs = (
        P(None, ("group", "leaf")),
        P(("group", "leaf"), None, None),
        P(("group", "leaf"), None),
        P(("group", "leaf")),
        P(("group", "leaf"), None),
        P(("group", "leaf"), None),
        P(("group", "leaf"), None, None),
        P(("group", "leaf"), None),
        P(("group", "leaf"), None),
        P(("group", "leaf"), None, None),
        P(("group", "leaf"), None),
        P("group", None, None),
    )
    out_specs = P(None, ("group", "leaf"))
    return jax.shard_map(
        per_device, mesh=mesh, in_specs=in_specs, out_specs=out_specs, check_vma=False
    )
```

profile of v0, /device:TPU:0, one launch (start us, length us, event | category | flops | bytes accessed | tf_op | source)
XLA Modules:
  0.0 376.4 jit_solution(737260132806493097)
XLA Ops:
  0.0 1.4 collective-permute-start.1
  1.4 3.7 collective-permute-start
  5.2 1.1 reshape.73
  6.3 1.5 reshape.72
  7.8 2.0 fusion.15
  10.0 0.9 reshape.74
  10.9 1.3 collective-permute-start.3
  12.2 3.7 collective-permute-start.2
  16.1 0.9 copy.85
  17.0 1.7 bitcast_reduce_fusion
  18.9 60.3 %all-gather = f32[64,4,512]{2,1,0:T(4,128)S(1)} all-gather(f32[1,4,512]{2,1,0:T(4,128)S(1)} %reshape.105), channel_id=1, replica_groups=mesh['group'=4,'leaf'=64] {'leaf'}, dimensions={0}, use_global_device_ids=true | all-gather | bytes 532480 | tf_op jit(solution)/shard_map/all_gather | solution.py:81
  79.2 1.0 reshape.112
  80.2 1.4 fusion.18
  81.8 1.1 reshape.80
  83.3 126.7 %psum.7 = f32[1,512]{1,0:T(1,128)S(1)} all-reduce(f32[1,512]{1,0:T(1,128)S(1)} %reshape.82), channel_id=1, replica_groups=mesh['group'=4,'leaf'=64] {'leaf'}, use_global_device_ids=true, to_apply=%region_4.5 | all-reduce | flops 512 | bytes 4096 | tf_op jit(solution)/shard_map/psum | solution.py:91
  209.9 11.2 %all-gather.1 = f32[4,1,512]{2,1,0:T(1,128)S(1)} all-gather(f32[1,1,512]{2,1,0:T(1,128)S(1)} %bitcast.75), channel_id=1, replica_groups=mesh['group'=4,'leaf'=64] {'group'}, dimensions={0}, use_global_device_ids=true | all-gather | bytes 10240 | tf_op jit(solution)/shard_map/all_gather | solution.py:92
  221.4 1.0 convolution_bitcast_fusion.1
  222.9 3.8 %copy.82 = f32[64,8,1024]{0,2,1:T(8,128)} copy(f32[64,8,1024]{2,1,0:T(8,128)} %param.20) | data formatting | bytes 4194304 | tf_op args[6]
  226.7 9.1 %copy.83 = f32[64,8,32,32]{3,2,1,0:T(8,128)} copy(f32[64,8,32,32]{0,3,2,1:T(8,128)} %bitcast.67) | data formatting | bytes 4194304 | tf_op jit(solution)/shard_map/reshape | solution.py:72
  236.8 1.1 concatenate.13
  237.9 1.2 copy.80
  239.0 1.1 concatenate.12
  240.4 1.1 pad_maximum_fusion
  241.6 3.1 gather_fusion.1
  244.6 10.6 %fusion.10 = f32[64,16,32]{2,1,0:T(8,128)S(1)} fusion(f32[64,8,32,32]{3,2,1,0:T(8,128)} %copy.83, f32[64,8,16,32]{3,2,1,0:T(8,128)} %bitcast.68, pred[64,8]{1,0:T(8,128)(4,1)S(1)} %copy.76), kind=kOutput, calls=%fused_computation.19 | convolution fusion | flops 100925440 | bytes 3277312 | tf_op jit(solution)/shard_map/tjkl,rtjl->tkr/dot_general | solution.py:70
  255.3 1.8 convolution_add_fusion.1
  257.1 1.0 pad_maximum_fusion.1
  258.7 2.1 copy.74
  260.8 0.8 broadcast_in_dim.31
  261.6 111.1 %while.10 = (s32[]{:T(128)}, f32[64,16,64]{2,1,0:T(8,128)}, s32[]{:T(128)}, s32[64,8]{0,1:T(8,128)S(1)}, f32[192,16,64]{2,1,0:T(8,128)}, /*index=5*/f32[64,8,409...) while((s32[]{:T(128)}, f32[64,16,64]{2,1,0:T(8,128)}, s32[]{:T(128)}, ...), condition=%wide.region_2.0_spmd, body=%wide.region_1.2_spmd.sunk | while | flops 50529796 | bytes 8656923 | solution.py:65
  262.4 4.4 %constant_dynamic-slice_fusion.2 = f32[64,1,4096]{2,1,0:T(1,128)S(1)} fusion(f32[64,8,4096]{2,1,0:T(8,128)} %get-tuple-element.170, s32[]{:T(128)S(6)} %select_n.43), kind=kLoop, calls=%fused_computation.11.clone.1 | loop fusion | bytes 2097156 | tf_op jit(solution)/shard_map/while/body/jit(dynamic_index_in_dim)/dynamic_slice | solution.py:58
  267.5 0.8 reshape.124
  268.4 2.0 gather_fusion
  270.4 5.3 %fusion.45 = f32[64,16,64]{2,1,0:T(8,128)} fusion(f32[64,16,64]{2,1,0:T(8,128)} %get-tuple-element.156, f32[64,64,64]{2,1,0:T(8,128)S(1)} %reshape.124, f32[64,16,64]{2,1,0:T(8,128)S(1)} %gather_fusion, f32[64]{0:T(128)S(1)} %compare_convert_fusion.2, pred[64]{0:T(512)(128)(4,1)S(1)} %get-tuple-element.144), kind=kOutput, calls=%fused_computation.3.clone.1 | convolution fusion | flops 50528256 | bytes 1835328 | tf_op jit(solution)/shard_map/while/body/tab,trb->tra/dot_general | solution.py:62
  276.2 4.4 %constant_dynamic-slice_fusion.2 = f32[64,1,4096]{2,1,0:T(1,128)S(1)} fusion(f32[64,8,4096]{2,1,0:T(8,128)} %get-tuple-element.170, s32[]{:T(128)S(6)} %select_n.43), kind=kLoop, calls=%fused_computation.11.clone.1 | loop fusion | bytes 2097156 | tf_op jit(solution)/shard_map/while/body/jit(dynamic_index_in_dim)/dynamic_slice | solution.py:58
  281.3 0.8 reshape.124
  282.2 2.0 gather_fusion
  284.2 5.3 %fusion.45 = f32[64,16,64]{2,1,0:T(8,128)} fusion(f32[64,16,64]{2,1,0:T(8,128)} %get-tuple-element.156, f32[64,64,64]{2,1,0:T(8,128)S(1)} %reshape.124, f32[64,16,64]{2,1,0:T(8,128)S(1)} %gather_fusion, f32[64]{0:T(128)S(1)} %compare_convert_fusion.2, pred[64]{0:T(512)(128)(4,1)S(1)} %get-tuple-element.144), kind=kOutput, calls=%fused_computation.3.clone.1 | convolution fusion | flops 50528256 | bytes 1835328 | tf_op jit(solution)/shard_map/while/body/tab,trb->tra/dot_general | solution.py:62
  290.0 4.4 %constant_dynamic-slice_fusion.2 = f32[64,1,4096]{2,1,0:T(1,128)S(1)} fusion(f32[64,8,4096]{2,1,0:T(8,128)} %get-tuple-element.170, s32[]{:T(128)S(6)} %select_n.43), kind=kLoop, calls=%fused_computation.11.clone.1 | loop fusion | bytes 2097156 | tf_op jit(solution)/shard_map/while/body/jit(dynamic_index_in_dim)/dynamic_slice | solution.py:58
  295.1 0.8 reshape.124
  295.9 2.0 gather_fusion
  298.0 5.3 %fusion.45 = f32[64,16,64]{2,1,0:T(8,128)} fusion(f32[64,16,64]{2,1,0:T(8,128)} %get-tuple-element.156, f32[64,64,64]{2,1,0:T(8,128)S(1)} %reshape.124, f32[64,16,64]{2,1,0:T(8,128)S(1)} %gather_fusion, f32[64]{0:T(128)S(1)} %compare_convert_fusion.2, pred[64]{0:T(512)(128)(4,1)S(1)} %get-tuple-element.144), kind=kOutput, calls=%fused_computation.3.clone.1 | convolution fusion | flops 50528256 | bytes 1835328 | tf_op jit(solution)/shard_map/while/body/tab,trb->tra/dot_general | solution.py:62
  303.8 4.4 %constant_dynamic-slice_fusion.2 = f32[64,1,4096]{2,1,0:T(1,128)S(1)} fusion(f32[64,8,4096]{2,1,0:T(8,128)} %get-tuple-element.170, s32[]{:T(128)S(6)} %select_n.43), kind=kLoop, calls=%fused_computation.11.clone.1 | loop fusion | bytes 2097156 | tf_op jit(solution)/shard_map/while/body/jit(dynamic_index_in_dim)/dynamic_slice | solution.py:58
  308.9 0.8 reshape.124
  309.7 2.0 gather_fusion
  311.8 5.3 %fusion.45 = f32[64,16,64]{2,1,0:T(8,128)} fusion(f32[64,16,64]{2,1,0:T(8,128)} %get-tuple-element.156, f32[64,64,64]{2,1,0:T(8,128)S(1)} %reshape.124, f32[64,16,64]{2,1,0:T(8,128)S(1)} %gather_fusion, f32[64]{0:T(128)S(1)} %compare_convert_fusion.2, pred[64]{0:T(512)(128)(4,1)S(1)} %get-tuple-element.144), kind=kOutput, calls=%fused_computation.3.clone.1 | convolution fusion | flops 50528256 | bytes 1835328 | tf_op jit(solution)/shard_map/while/body/tab,trb->tra/dot_general | solution.py:62
  317.6 4.4 %constant_dynamic-slice_fusion.2 = f32[64,1,4096]{2,1,0:T(1,128)S(1)} fusion(f32[64,8,4096]{2,1,0:T(8,128)} %get-tuple-element.170, s32[]{:T(128)S(6)} %select_n.43), kind=kLoop, calls=%fused_computation.11.clone.1 | loop fusion | bytes 2097156 | tf_op jit(solution)/shard_map/while/body/jit(dynamic_index_in_dim)/dynamic_slice | solution.py:58
  322.7 0.8 reshape.124
  323.5 2.0 gather_fusion
  325.5 5.3 %fusion.45 = f32[64,16,64]{2,1,0:T(8,128)} fusion(f32[64,16,64]{2,1,0:T(8,128)} %get-tuple-element.156, f32[64,64,64]{2,1,0:T(8,128)S(1)} %reshape.124, f32[64,16,64]{2,1,0:T(8,128)S(1)} %gather_fusion, f32[64]{0:T(128)S(1)} %compare_convert_fusion.2, pred[64]{0:T(512)(128)(4,1)S(1)} %get-tuple-element.144), kind=kOutput, calls=%fused_computation.3.clone.1 | convolution fusion | flops 50528256 | bytes 1835328 | tf_op jit(solution)/shard_map/while/body/tab,trb->tra/dot_general | solution.py:62
  331.4 4.4 %constant_dynamic-slice_fusion.2 = f32[64,1,4096]{2,1,0:T(1,128)S(1)} fusion(f32[64,8,4096]{2,1,0:T(8,128)} %get-tuple-element.170, s32[]{:T(128)S(6)} %select_n.43), kind=kLoop, calls=%fused_computation.11.clone.1 | loop fusion | bytes 2097156 | tf_op jit(solution)/shard_map/while/body/jit(dynamic_index_in_dim)/dynamic_slice | solution.py:58
  336.4 0.8 reshape.124
  337.3 2.0 gather_fusion
  339.3 5.3 %fusion.45 = f32[64,16,64]{2,1,0:T(8,128)} fusion(f32[64,16,64]{2,1,0:T(8,128)} %get-tuple-element.156, f32[64,64,64]{2,1,0:T(8,128)S(1)} %reshape.124, f32[64,16,64]{2,1,0:T(8,128)S(1)} %gather_fusion, f32[64]{0:T(128)S(1)} %compare_convert_fusion.2, pred[64]{0:T(512)(128)(4,1)S(1)} %get-tuple-element.144), kind=kOutput, calls=%fused_computation.3.clone.1 | convolution fusion | flops 50528256 | bytes 1835328 | tf_op jit(solution)/shard_map/while/body/tab,trb->tra/dot_general | solution.py:62
  345.2 4.4 %constant_dynamic-slice_fusion.2 = f32[64,1,4096]{2,1,0:T(1,128)S(1)} fusion(f32[64,8,4096]{2,1,0:T(8,128)} %get-tuple-element.170, s32[]{:T(128)S(6)} %select_n.43), kind=kLoop, calls=%fused_computation.11.clone.1 | loop fusion | bytes 2097156 | tf_op jit(solution)/shard_map/while/body/jit(dynamic_index_in_dim)/dynamic_slice | solution.py:58
  350.2 0.8 reshape.124
  351.1 2.0 gather_fusion
  353.1 5.3 %fusion.45 = f32[64,16,64]{2,1,0:T(8,128)} fusion(f32[64,16,64]{2,1,0:T(8,128)} %get-tuple-element.156, f32[64,64,64]{2,1,0:T(8,128)S(1)} %reshape.124, f32[64,16,64]{2,1,0:T(8,128)S(1)} %gather_fusion, f32[64]{0:T(128)S(1)} %compare_convert_fusion.2, pred[64]{0:T(512)(128)(4,1)S(1)} %get-tuple-element.144), kind=kOutput, calls=%fused_computation.3.clone.1 | convolution fusion | flops 50528256 | bytes 1835328 | tf_op jit(solution)/shard_map/while/body/tab,trb->tra/dot_general | solution.py:62
  359.0 4.4 %constant_dynamic-slice_fusion.2 = f32[64,1,4096]{2,1,0:T(1,128)S(1)} fusion(f32[64,8,4096]{2,1,0:T(8,128)} %get-tuple-element.170, s32[]{:T(128)S(6)} %select_n.43), kind=kLoop, calls=%fused_computation.11.clone.1 | loop fusion | bytes 2097156 | tf_op jit(solution)/shard_map/while/body/jit(dynamic_index_in_dim)/dynamic_slice | solution.py:58
  364.0 0.8 reshape.124
  364.9 2.0 gather_fusion
  366.9 5.3 %fusion.45 = f32[64,16,64]{2,1,0:T(8,128)} fusion(f32[64,16,64]{2,1,0:T(8,128)} %get-tuple-element.156, f32[64,64,64]{2,1,0:T(8,128)S(1)} %reshape.124, f32[64,16,64]{2,1,0:T(8,128)S(1)} %gather_fusion, f32[64]{0:T(128)S(1)} %compare_convert_fusion.2, pred[64]{0:T(512)(128)(4,1)S(1)} %get-tuple-element.144), kind=kOutput, calls=%fused_computation.3.clone.1 | convolution fusion | flops 50528256 | bytes 1835328 | tf_op jit(solution)/shard_map/while/body/tab,trb->tra/dot_general | solution.py:62
  372.7 2.6 fusion.13
  375.5 0.9 reshape.86
  (79 shorter events, 9.0 us)
Async XLA Ops:
  0.0 15.8 %copy-start.2 = (f32[64,1024]{1,0:T(8,128)S(1)}, f32[64,1024]{1,0:T(8,128)}, u32[]{:S(2)}) copy-start(f32[64,1024]{1,0:T(8,128)} %param.21) | copy-start | bytes 786436
  0.0 257.1 %collective-permute-start.1 = (f32[16,4096]{1,0:T(8,128)}, f32[16,4096]{1,0:T(8,128)S(1)}, u32[]{:S(2)}, u32[]{:S(2)}) collective-permute-start(f32[16,4096]{1,0:T(8,128)} %param.14), channel_id=1, source_target_pairs={{1,0},{2,1},{3,2},{4,3},{5,4},{6,5},{7,6},{8,7},{9,8},{10,9},{11,1... | collective-permute-start | bytes 786440 | tf_op jit(solution)/shard_map/ppermute | solution.py:22
  1.4 255.7 %collective-permute-start = (f32[16,4096]{1,0:T(8,128)}, f32[16,4096]{1,0:T(8,128)}, u32[]{:S(2)}, u32[]{:S(2)}) collective-permute-start(f32[16,4096]{1,0:T(8,128)} %param.14), channel_id=1, source_target_pairs={{0,1},{1,2},{2,3},{3,4},{4,5},{5,6},{6,7},{7,8},{8,9},{9,10},{10,1... | collective-permute-start | bytes 786440 | tf_op jit(solution)/shard_map/ppermute | solution.py:21
  7.8 71.4 %copy-start = (f32[64,32,64]{2,1,0:T(8,128)}, f32[64,32,64]{2,1,0:T(8,128)S(1)}, u32[]{:S(2)}) copy-start(f32[64,32,64]{2,1,0:T(8,128)S(1)} %reshape.72) | copy-start | bytes 1572868
  9.7 70.4 %copy-start.7 = (s32[4,8]{1,0:T(4,128)S(1)}, s32[4,8]{1,0:T(4,128)}, u32[]{:S(2)}) copy-start(s32[4,8]{1,0:T(4,128)} %param.22) | copy-start | bytes 388
  9.9 72.9 %copy-start.3 = (f32[4,1024]{1,0:T(4,128)S(1)}, f32[4,1024]{1,0:T(4,128)}, u32[]{:S(2)}) copy-start(f32[4,1024]{1,0:T(4,128)} %param.24) | copy-start | bytes 49156
  9.9 211.4 %copy-start.4 = (f32[1,4,1024]{2,1,0:T(4,128)S(1)}, f32[1,4,1024]{2,1,0:T(4,128)}, u32[]{:S(2)}) copy-start(f32[1,4,1024]{2,1,0:T(4,128)} %param.25) | copy-start | bytes 49156
  10.0 211.4 %copy-start.5 = (s32[64,8]{0,1:T(8,128)S(1)}, s32[64,8]{0,1:T(8,128)}, u32[]{:S(2)}) copy-start(s32[64,8]{0,1:T(8,128)} %param.19) | copy-start | bytes 6148
  10.9 225.9 %collective-permute-start.3 = (f32[16,2048]{1,0:T(8,128)}, f32[16,2048]{1,0:T(8,128)}, u32[]{:S(2)}, u32[]{:S(2)}) collective-permute-start(f32[16,2048]{1,0:T(8,128)} %reshape.74), channel_id=1, source_target_pairs={{1,0},{2,1},{3,2},{4,3},{5,4},{6,5},{7,6},{8,7},{9,8},{10,9},{11,1... | collective-permute-start | bytes 393224 | tf_op jit(solution)/shard_map/ppermute | solution.py:22
  12.2 226.9 %collective-permute-start.2 = (f32[16,2048]{1,0:T(8,128)}, f32[16,2048]{1,0:T(8,128)}, u32[]{:S(2)}, u32[]{:S(2)}) collective-permute-start(f32[16,2048]{1,0:T(8,128)} %reshape.74), channel_id=1, source_target_pairs={{0,1},{1,2},{2,3},{3,4},{4,5},{5,6},{6,7},{7,8},{8,9},{9,10},{10,1... | collective-permute-start | bytes 393224 | tf_op jit(solution)/shard_map/ppermute | solution.py:21
  16.0 206.8 %copy-start.6 = (s32[64,8]{0,1:T(8,128)S(1)}, s32[64,8]{0,1:T(8,128)}, u32[]{:S(2)}) copy-start(s32[64,8]{0,1:T(8,128)} %param.16) | copy-start | bytes 6148
  226.7 9.4 %copy-start.8 = (s32[64]{0:T(128)S(1)}, s32[64]{0:T(128)}, u32[]{:S(2)}) copy-start(s32[64]{0:T(128)} %param.17) | copy-start | bytes 772
  244.6 12.5 %copy-start.1 = (f32[16,4096]{1,0:T(8,128)S(1)}, f32[16,4096]{1,0:T(8,128)}, u32[]{:S(2)}) copy-start(f32[16,4096]{1,0:T(8,128)} %param.14) | copy-start | bytes 786436
where the time goes:
time: 378 us; the launch traced here: 376 us
  blocking collectives  198 us (52%)
  local copies, waits for them, and re-layouts  95.3 us (25%)
  matrix products  63.6 us (17%)
  starting transfers between devices  10.1 us (3%)
  loops' own time  5.86 us (2%)
    psum x1, blocking collectives, per_device(): group_sum = lax.psum(projected_sum, 'leaf')  127 us
    all_gather x1, blocking collectives, per_device(): shard_rows = lax.all_gather(cluster_rows, 'leaf', axis=0, tiled=True)  60.3 us
    dot_general x8, matrix products, near_step(): term = jnp.einsum('tab,trb->tra', slab, picked, precision=highest_precision)  42 us
    dynamic_slice x16, local copies, waits for them, and re-layouts, near_step(): lax.dynamic_index_in_dim(near_blocks, slot_index, axis=1, keepdims=False)  40.3 us
    gather x8, local copies, waits for them, and re-layouts, near_step(): picked = jnp.take(point_blocks, near_local[:, slot_index], axis=0)  16 us
    all_gather x1, blocking collectives, per_device(): all_groups = lax.all_gather(group_sum, 'group', axis=0, tiled=True)  11.2 us
    dot_general x1, matrix products, per_device(): jnp.einsum('tjkl,rtjl->tkr', leaf_coupling.reshape(leaves_here, FAR0, K,...  10.6 us
    reshape x1, local copies, waits for them, and re-layouts, per_device(): leaf_coupling.reshape(leaves_here, FAR0, K, K)  9.12 us
  transfers between devices with their start and end apart: 4, of which 0 were waited for; matrix products, arithmetic and copies ran while one was open for 13% of the time, Pallas kernels for 0%

commit v1 on v0

--- a/solution.py
+++ b/solution.py
@@ -1,3 +1,4 @@
+import functools
 import jax
 import jax.numpy as jnp
 from jax import lax
@@ -9,6 +10,21 @@
 FAR0 = 8
 FAR1 = 8
 highest_precision = lax.Precision.HIGHEST
+
+
+def ports_place(inner_x, bus_axis):
+    slots = jax.lax.axis_size(bus_axis)
+    g_now = [(b - 1, b) for b in range(1, slots)] + [(slots - 1, 0)]
+    o_now = inner_x
+    pile = [o_now]
+    for _ in range(slots - 1):
+        o_now = jax.lax.ppermute(o_now, axis_name=bus_axis, perm=g_now)
+        pile += [o_now]
+    arr_out = jnp.concatenate([*reversed(pile)], 0)
+    return jnp.roll(arr_out, (jax.lax.axis_index(bus_axis) + 1) * o_now.shape[0], 0)
+
+
+extend_local_data = functools.partial(ports_place, bus_axis="group")
 
 
 def extended(value, sides, width):
@@ -89,7 +105,7 @@
     projected = jnp.einsum("ukl,ulr->ukr", upper, cluster_coef, precision=highest_precision)
     projected_sum = projected.sum(axis=0).reshape(1, K * RHS)
     group_sum = lax.psum(projected_sum, "leaf")
-    all_groups = lax.all_gather(group_sum, "group", axis=0, tiled=True)
+    all_groups = extend_local_data(group_sum)
     group_field = jnp.einsum(
         "hkl,hlr->kr",
         group_coupling.reshape(ngroups, K, K),

time: 378 us -> 378 us (level)
  blocking collectives: 198 us -> 191 us
    psum x1, blocking collectives: 127 us -> 140 us  [per_device(): group_sum = lax.psum(projected_sum, 'leaf')]
    all_gather x1 -> x0, blocking collectives: 11.2 us -> none  [per_device(): all_groups = lax.all_gather(group_sum, 'group', axis=0, tiled=True)]
    all_gather x1, blocking collectives: 60.3 us -> 51.8 us  [per_device(): shard_rows = lax.all_gather(cluster_rows, 'leaf', axis=0, tiled=True)]
  transfers between devices with their start and end apart: 4 -> 7, of which waited for: 0 -> 1; matrix products, arithmetic and copies ran while one was open for 13% -> 13% of each run, Pallas kernels for 0% -> 0%
where the time goes in v1:
time: 378 us; the launch traced here: 376 us
  blocking collectives  191 us (51%)
  local copies, waits for them, and re-layouts  95.6 us (25%)
  matrix products  62.7 us (17%)
  starting transfers between devices  13.5 us (4%)
  loops' own time  7.01 us (2%)
    psum x1, blocking collectives, per_device(): group_sum = lax.psum(projected_sum, 'leaf')  140 us
    all_gather x1, blocking collectives, per_device(): shard_rows = lax.all_gather(cluster_rows, 'leaf', axis=0, tiled=True)  51.8 us
    dot_general x8, matrix products, near_step(): term = jnp.einsum('tab,trb->tra', slab, picked, precision=highest_precision)  42.1 us
    dynamic_slice x16, local copies, waits for them, and re-layouts, near_step(): lax.dynamic_index_in_dim(near_blocks, slot_index, axis=1, keepdims=False)  40.3 us
    gather x8, local copies, waits for them, and re-layouts, near_step(): picked = jnp.take(point_blocks, near_local[:, slot_index], axis=0)  16 us
    dot_general x1, matrix products, per_device(): jnp.einsum('tjkl,rtjl->tkr', leaf_coupling.reshape(leaves_here, FAR0, K,...  10.6 us
    reshape x1, local copies, waits for them, and re-layouts, per_device(): leaf_coupling.reshape(leaves_here, FAR0, K, K)  9.18 us
  transfers between devices with their start and end apart: 7, of which 1 were waited for; matrix products, arithmetic and copies ran while one was open for 13% of the time, Pallas kernels for 0%

profile of v1, /device:TPU:0, one launch (start us, length us, event | category | flops | bytes accessed | tf_op | source)
XLA Modules:
  0.0 375.9 jit_solution(11243140613233326289)
XLA Ops:
  0.0 1.4 collective-permute-start.1
  1.4 3.7 collective-permute-start
  5.2 1.1 reshape.73
  6.3 1.5 reshape.72
  7.8 2.0 fusion.15
  10.0 0.9 reshape.74
  10.9 1.3 collective-permute-start.3
  12.2 3.7 collective-permute-start.2
  16.1 0.9 copy.85
  17.0 1.7 bitcast_reduce_fusion
  19.2 139.6 %psum.7 = f32[1,512]{1,0:T(1,128)S(1)} all-reduce(f32[1,512]{1,0:T(1,128)S(1)} %reshape.82), channel_id=1, replica_groups=mesh['group'=4,'leaf'=64] {'leaf'}, use_global_device_ids=true, to_apply=%region_4.5 | all-reduce | flops 512 | bytes 4096 | tf_op jit(solution)/shard_map/psum | solution.py:107
  158.8 1.5 collective-permute-start.4
  160.5 51.8 %all-gather = f32[64,4,512]{2,1,0:T(4,128)} all-gather(f32[1,4,512]{2,1,0:T(4,128)S(1)} %reshape.105), channel_id=1, replica_groups=mesh['group'=4,'leaf'=64] {'leaf'}, dimensions={0}, use_global_device_ids=true | all-gather | bytes 532480 | tf_op jit(solution)/shard_map/all_gather | solution.py:97
  212.4 1.2 reshape.109
  214.2 1.1 reshape.80
  215.3 1.6 collective-permute-start.5
  216.9 1.0 convolution_bitcast_fusion.1
  218.0 2.1 collective-permute-done.5
  220.4 3.8 %copy.82 = f32[64,8,1024]{0,2,1:T(8,128)} copy(f32[64,8,1024]{2,1,0:T(8,128)} %param.20) | data formatting | bytes 4194304 | tf_op args[6]
  224.3 9.2 %copy.83 = f32[64,8,32,32]{3,2,1,0:T(8,128)} copy(f32[64,8,32,32]{0,3,2,1:T(8,128)} %bitcast.66) | data formatting | bytes 4194304 | tf_op jit(solution)/shard_map/reshape | solution.py:88
  235.0 1.1 concatenate.19
  236.1 1.1 copy.80
  237.2 1.1 concatenate.18
  238.6 1.1 pad_maximum_fusion
  239.8 3.1 gather_fusion.1
  242.9 10.6 %fusion.10 = f32[64,16,32]{2,1,0:T(8,128)S(1)} fusion(f32[64,8,32,32]{3,2,1,0:T(8,128)} %copy.83, f32[64,8,16,32]{3,2,1,0:T(8,128)} %bitcast.67, pred[64,8]{1,0:T(8,128)(4,1)S(1)} %copy.76), kind=kOutput, calls=%fused_computation.19 | convolution fusion | flops 100925440 | bytes 3277312 | tf_op jit(solution)/shard_map/tjkl,rtjl->tkr/dot_general | solution.py:86
  253.5 1.8 convolution_add_fusion.1
  255.4 1.0 pad_maximum_fusion.1
  257.0 2.1 copy.74
  259.1 0.8 broadcast_in_dim.31
  259.9 112.3 %while.10 = (s32[]{:T(128)}, f32[64,16,64]{2,1,0:T(8,128)}, s32[]{:T(128)}, s32[64,8]{0,1:T(8,128)S(1)}, f32[192,16,64]{2,1,0:T(8,128)}, /*index=5*/f32[64,8,409...) while((s32[]{:T(128)}, f32[64,16,64]{2,1,0:T(8,128)}, s32[]{:T(128)}, ...), condition=%wide.region_2.0_spmd, body=%wide.region_1.2_spmd.sunk | while | flops 50529796 | bytes 8656923 | solution.py:81
  260.8 4.4 %constant_dynamic-slice_fusion.3 = f32[64,1,4096]{2,1,0:T(1,128)S(1)} fusion(f32[64,8,4096]{2,1,0:T(8,128)} %get-tuple-element.170, s32[]{:T(128)S(6)} %select_n.58), kind=kLoop, calls=%fused_computation.11.clone.1 | loop fusion | bytes 2097156 | tf_op jit(solution)/shard_map/while/body/jit(dynamic_index_in_dim)/dynamic_slice | solution.py:74
  265.9 0.8 reshape.120
  266.8 2.0 gather_fusion
  268.8 5.3 %fusion.45 = f32[64,16,64]{2,1,0:T(8,128)} fusion(f32[64,16,64]{2,1,0:T(8,128)} %get-tuple-element.156, f32[64,64,64]{2,1,0:T(8,128)S(1)} %reshape.120, f32[64,16,64]{2,1,0:T(8,128)S(1)} %gather_fusion, f32[64]{0:T(128)S(1)} %compare_convert_fusion.2, pred[64]{0:T(512)(128)(4,1)S(1)} %get-tuple-element.144), kind=kOutput, calls=%fused_computation.3.clone.1 | convolution fusion | flops 50528256 | bytes 1835328 | tf_op jit(solution)/shard_map/while/body/tab,trb->tra/dot_general | solution.py:78
  274.8 4.4 %constant_dynamic-slice_fusion.3 = f32[64,1,4096]{2,1,0:T(1,128)S(1)} fusion(f32[64,8,4096]{2,1,0:T(8,128)} %get-tuple-element.170, s32[]{:T(128)S(6)} %select_n.58), kind=kLoop, calls=%fused_computation.11.clone.1 | loop fusion | bytes 2097156 | tf_op jit(solution)/shard_map/while/body/jit(dynamic_index_in_dim)/dynamic_slice | solution.py:74
  279.8 0.8 reshape.120
  280.7 2.0 gather_fusion
  282.7 5.3 %fusion.45 = f32[64,16,64]{2,1,0:T(8,128)} fusion(f32[64,16,64]{2,1,0:T(8,128)} %get-tuple-element.156, f32[64,64,64]{2,1,0:T(8,128)S(1)} %reshape.120, f32[64,16,64]{2,1,0:T(8,128)S(1)} %gather_fusion, f32[64]{0:T(128)S(1)} %compare_convert_fusion.2, pred[64]{0:T(512)(128)(4,1)S(1)} %get-tuple-element.144), kind=kOutput, calls=%fused_computation.3.clone.1 | convolution fusion | flops 50528256 | bytes 1835328 | tf_op jit(solution)/shard_map/while/body/tab,trb->tra/dot_general | solution.py:78
  288.7 4.4 %constant_dynamic-slice_fusion.3 = f32[64,1,4096]{2,1,0:T(1,128)S(1)} fusion(f32[64,8,4096]{2,1,0:T(8,128)} %get-tuple-element.170, s32[]{:T(128)S(6)} %select_n.58), kind=kLoop, calls=%fused_computation.11.clone.1 | loop fusion | bytes 2097156 | tf_op jit(solution)/shard_map/while/body/jit(dynamic_index_in_dim)/dynamic_slice | solution.py:74
  293.7 0.8 reshape.120
  294.6 2.0 gather_fusion
  296.6 5.3 %fusion.45 = f32[64,16,64]{2,1,0:T(8,128)} fusion(f32[64,16,64]{2,1,0:T(8,128)} %get-tuple-element.156, f32[64,64,64]{2,1,0:T(8,128)S(1)} %reshape.120, f32[64,16,64]{2,1,0:T(8,128)S(1)} %gather_fusion, f32[64]{0:T(128)S(1)} %compare_convert_fusion.2, pred[64]{0:T(512)(128)(4,1)S(1)} %get-tuple-element.144), kind=kOutput, calls=%fused_computation.3.clone.1 | convolution fusion | flops 50528256 | bytes 1835328 | tf_op jit(solution)/shard_map/while/body/tab,trb->tra/dot_general | solution.py:78
  302.6 4.4 %constant_dynamic-slice_fusion.3 = f32[64,1,4096]{2,1,0:T(1,128)S(1)} fusion(f32[64,8,4096]{2,1,0:T(8,128)} %get-tuple-element.170, s32[]{:T(128)S(6)} %select_n.58), kind=kLoop, calls=%fused_computation.11.clone.1 | loop fusion | bytes 2097156 | tf_op jit(solution)/shard_map/while/body/jit(dynamic_index_in_dim)/dynamic_slice | solution.py:74
  307.7 0.8 reshape.120
  308.6 2.0 gather_fusion
  310.6 5.3 %fusion.45 = f32[64,16,64]{2,1,0:T(8,128)} fusion(f32[64,16,64]{2,1,0:T(8,128)} %get-tuple-element.156, f32[64,64,64]{2,1,0:T(8,128)S(1)} %reshape.120, f32[64,16,64]{2,1,0:T(8,128)S(1)} %gather_fusion, f32[64]{0:T(128)S(1)} %compare_convert_fusion.2, pred[64]{0:T(512)(128)(4,1)S(1)} %get-tuple-element.144), kind=kOutput, calls=%fused_computation.3.clone.1 | convolution fusion | flops 50528256 | bytes 1835328 | tf_op jit(solution)/shard_map/while/body/tab,trb->tra/dot_general | solution.py:78
  316.6 4.4 %constant_dynamic-slice_fusion.3 = f32[64,1,4096]{2,1,0:T(1,128)S(1)} fusion(f32[64,8,4096]{2,1,0:T(8,128)} %get-tuple-element.170, s32[]{:T(128)S(6)} %select_n.58), kind=kLoop, calls=%fused_computation.11.clone.1 | loop fusion | bytes 2097156 | tf_op jit(solution)/shard_map/while/body/jit(dynamic_index_in_dim)/dynamic_slice | solution.py:74
  321.6 0.8 reshape.120
  322.5 2.0 gather_fusion
  324.5 5.3 %fusion.45 = f32[64,16,64]{2,1,0:T(8,128)} fusion(f32[64,16,64]{2,1,0:T(8,128)} %get-tuple-element.156, f32[64,64,64]{2,1,0:T(8,128)S(1)} %reshape.120, f32[64,16,64]{2,1,0:T(8,128)S(1)} %gather_fusion, f32[64]{0:T(128)S(1)} %compare_convert_fusion.2, pred[64]{0:T(512)(128)(4,1)S(1)} %get-tuple-element.144), kind=kOutput, calls=%fused_computation.3.clone.1 | convolution fusion | flops 50528256 | bytes 1835328 | tf_op jit(solution)/shard_map/while/body/tab,trb->tra/dot_general | solution.py:78
  330.5 4.4 %constant_dynamic-slice_fusion.3 = f32[64,1,4096]{2,1,0:T(1,128)S(1)} fusion(f32[64,8,4096]{2,1,0:T(8,128)} %get-tuple-element.170, s32[]{:T(128)S(6)} %select_n.58), kind=kLoop, calls=%fused_computation.11.clone.1 | loop fusion | bytes 2097156 | tf_op jit(solution)/shard_map/while/body/jit(dynamic_index_in_dim)/dynamic_slice | solution.py:74
  335.5 0.8 reshape.120
  336.4 2.0 gather_fusion
  338.4 5.3 %fusion.45 = f32[64,16,64]{2,1,0:T(8,128)} fusion(f32[64,16,64]{2,1,0:T(8,128)} %get-tuple-element.156, f32[64,64,64]{2,1,0:T(8,128)S(1)} %reshape.120, f32[64,16,64]{2,1,0:T(8,128)S(1)} %gather_fusion, f32[64]{0:T(128)S(1)} %compare_convert_fusion.2, pred[64]{0:T(512)(128)(4,1)S(1)} %get-tuple-element.144), kind=kOutput, calls=%fused_computation.3.clone.1 | convolution fusion | flops 50528256 | bytes 1835328 | tf_op jit(solution)/shard_map/while/body/tab,trb->tra/dot_general | solution.py:78
  344.4 4.4 %constant_dynamic-slice_fusion.3 = f32[64,1,4096]{2,1,0:T(1,128)S(1)} fusion(f32[64,8,4096]{2,1,0:T(8,128)} %get-tuple-element.170, s32[]{:T(128)S(6)} %select_n.58), kind=kLoop, calls=%fused_computation.11.clone.1 | loop fusion | bytes 2097156 | tf_op jit(solution)/shard_map/while/body/jit(dynamic_index_in_dim)/dynamic_slice | solution.py:74
  350.3 2.0 gather_fusion
  352.4 5.3 %fusion.45 = f32[64,16,64]{2,1,0:T(8,128)} fusion(f32[64,16,64]{2,1,0:T(8,128)} %get-tuple-element.156, f32[64,64,64]{2,1,0:T(8,128)S(1)} %reshape.120, f32[64,16,64]{2,1,0:T(8,128)S(1)} %gather_fusion, f32[64]{0:T(128)S(1)} %compare_convert_fusion.2, pred[64]{0:T(512)(128)(4,1)S(1)} %get-tuple-element.144), kind=kOutput, calls=%fused_computation.3.clone.1 | convolution fusion | flops 50528256 | bytes 1835328 | tf_op jit(solution)/shard_map/while/body/tab,trb->tra/dot_general | solution.py:78
  358.3 4.4 %constant_dynamic-slice_fusion.3 = f32[64,1,4096]{2,1,0:T(1,128)S(1)} fusion(f32[64,8,4096]{2,1,0:T(8,128)} %get-tuple-element.170, s32[]{:T(128)S(6)} %select_n.58), kind=kLoop, calls=%fused_computation.11.clone.1 | loop fusion | bytes 2097156 | tf_op jit(solution)/shard_map/while/body/jit(dynamic_index_in_dim)/dynamic_slice | solution.py:74
  363.4 0.8 reshape.120
  364.3 2.0 gather_fusion
  366.3 5.3 %fusion.45 = f32[64,16,64]{2,1,0:T(8,128)} fusion(f32[64,16,64]{2,1,0:T(8,128)} %get-tuple-element.156, f32[64,64,64]{2,1,0:T(8,128)S(1)} %reshape.120, f32[64,16,64]{2,1,0:T(8,128)S(1)} %gather_fusion, f32[64]{0:T(128)S(1)} %compare_convert_fusion.2, pred[64]{0:T(512)(128)(4,1)S(1)} %get-tuple-element.144), kind=kOutput, calls=%fused_computation.3.clone.1 | convolution fusion | flops 50528256 | bytes 1835328 | tf_op jit(solution)/shard_map/while/body/tab,trb->tra/dot_general | solution.py:78
  372.3 2.6 fusion.13
  375.0 0.9 reshape.86
  (85 shorter events, 10.5 us)
Async XLA Ops:
  0.0 15.9 %copy-start.2 = (f32[64,1024]{1,0:T(8,128)S(1)}, f32[64,1024]{1,0:T(8,128)}, u32[]{:S(2)}) copy-start(f32[64,1024]{1,0:T(8,128)} %param.21) | copy-start | bytes 786436
  0.0 255.3 %collective-permute-start.1 = (f32[16,4096]{1,0:T(8,128)}, f32[16,4096]{1,0:T(8,128)S(1)}, u32[]{:S(2)}, u32[]{:S(2)}) collective-permute-start(f32[16,4096]{1,0:T(8,128)} %param.14), channel_id=1, source_target_pairs={{1,0},{2,1},{3,2},{4,3},{5,4},{6,5},{7,6},{8,7},{9,8},{10,9},{11,1... | collective-permute-start | bytes 786440 | tf_op jit(solution)/shard_map/ppermute | solution.py:38
  1.4 253.9 %collective-permute-start = (f32[16,4096]{1,0:T(8,128)}, f32[16,4096]{1,0:T(8,128)}, u32[]{:S(2)}, u32[]{:S(2)}) collective-permute-start(f32[16,4096]{1,0:T(8,128)} %param.14), channel_id=1, source_target_pairs={{0,1},{1,2},{2,3},{3,4},{4,5},{5,6},{6,7},{7,8},{8,9},{9,10},{10,1... | collective-permute-start | bytes 786440 | tf_op jit(solution)/shard_map/ppermute | solution.py:37
  7.8 204.6 %copy-start = (f32[64,32,64]{2,1,0:T(8,128)}, f32[64,32,64]{2,1,0:T(8,128)S(1)}, u32[]{:S(2)}) copy-start(f32[64,32,64]{2,1,0:T(8,128)S(1)} %reshape.72) | copy-start | bytes 1572868
  7.8 10.9 %copy-start.3 = (f32[4,1024]{1,0:T(4,128)S(1)}, f32[4,1024]{1,0:T(4,128)}, u32[]{:S(2)}) copy-start(f32[4,1024]{1,0:T(4,128)} %param.24) | copy-start | bytes 49156
  9.8 203.8 %copy-start.5 = (s32[64,8]{0,1:T(8,128)S(1)}, s32[64,8]{0,1:T(8,128)}, u32[]{:S(2)}) copy-start(s32[64,8]{0,1:T(8,128)} %param.19) | copy-start | bytes 6148
  9.8 203.8 %copy-start.7 = (s32[4,8]{1,0:T(4,128)S(1)}, s32[4,8]{1,0:T(4,128)}, u32[]{:S(2)}) copy-start(s32[4,8]{1,0:T(4,128)} %param.22) | copy-start | bytes 388
  9.8 204.2 %copy-start.6 = (s32[64,8]{0,1:T(8,128)S(1)}, s32[64,8]{0,1:T(8,128)}, u32[]{:S(2)}) copy-start(s32[64,8]{0,1:T(8,128)} %param.16) | copy-start | bytes 6148
  10.9 224.1 %collective-permute-start.3 = (f32[16,2048]{1,0:T(8,128)}, f32[16,2048]{1,0:T(8,128)}, u32[]{:S(2)}, u32[]{:S(2)}) collective-permute-start(f32[16,2048]{1,0:T(8,128)} %reshape.74), channel_id=1, source_target_pairs={{1,0},{2,1},{3,2},{4,3},{5,4},{6,5},{7,6},{8,7},{9,8},{10,9},{11,1... | collective-permute-start | bytes 393224 | tf_op jit(solution)/shard_map/ppermute | solution.py:38
  12.2 225.1 %collective-permute-start.2 = (f32[16,2048]{1,0:T(8,128)}, f32[16,2048]{1,0:T(8,128)}, u32[]{:S(2)}, u32[]{:S(2)}) collective-permute-start(f32[16,2048]{1,0:T(8,128)} %reshape.74), channel_id=1, source_target_pairs={{0,1},{1,2},{2,3},{3,4},{4,5},{5,6},{6,7},{7,8},{8,9},{9,10},{10,1... | collective-permute-start | bytes 393224 | tf_op jit(solution)/shard_map/ppermute | solution.py:37
  158.8 56.5 %collective-permute-start.4 = (f32[1,512]{1,0:T(1,128)S(1)}, f32[1,512]{1,0:T(1,128)S(1)}, u32[]{:S(2)}, u32[]{:S(2)}) collective-permute-start(f32[1,512]{1,0:T(1,128)S(1)} %psum.7), channel_id=1, source_target_pairs={{0,64},{64,128},{128,192},{192,0},{1,65},{65,129},{129,193},{193,1... | collective-permute-start | bytes 6152 | tf_op jit(solution)/shard_map/ppermute | solution.py:21
  215.3 4.9 %collective-permute-start.5 = (f32[1,512]{1,0:T(1,128)S(1)}, f32[1,512]{1,0:T(1,128)S(1)}, u32[]{:S(2)}, u32[]{:S(2)}) collective-permute-start(f32[1,512]{1,0:T(1,128)S(1)} %collective-permute-done.4), channel_id=1, source_target_pairs={{0,64},{64,128},{128,192},{192,0},{1,65},{65,129},{129,193},{193,1... | collective-permute-start | bytes 6152 | tf_op jit(solution)/shard_map/ppermute | solution.py:21
  220.2 14.2 %collective-permute-start.6 = (f32[1,512]{1,0:T(1,128)S(1)}, f32[1,512]{1,0:T(1,128)S(1)}, u32[]{:S(2)}, u32[]{:S(2)}) collective-permute-start(f32[1,512]{1,0:T(1,128)S(1)} %collective-permute-done.5), channel_id=1, source_target_pairs={{0,64},{64,128},{128,192},{192,0},{1,65},{65,129},{129,193},{193,1... | collective-permute-start | bytes 6152 | tf_op jit(solution)/shard_map/ppermute | solution.py:21
  224.3 9.3 %copy-start.4 = (f32[1,4,1024]{2,1,0:T(4,128)S(1)}, f32[1,4,1024]{2,1,0:T(4,128)}, u32[]{:S(2)}) copy-start(f32[1,4,1024]{2,1,0:T(4,128)} %param.25) | copy-start | bytes 49156
  224.3 9.4 %copy-start.8 = (s32[64]{0:T(128)S(1)}, s32[64]{0:T(128)}, u32[]{:S(2)}) copy-start(s32[64]{0:T(128)} %param.17) | copy-start | bytes 772
  242.9 12.5 %copy-start.1 = (f32[16,4096]{1,0:T(8,128)S(1)}, f32[16,4096]{1,0:T(8,128)}, u32[]{:S(2)}) copy-start(f32[16,4096]{1,0:T(8,128)} %param.14) | copy-start | bytes 786436
